TPU v7x, 32 devices: a whole 2x2x4 slice. The times are simulated.
32 devices in a mesh: row: 8 (over z, core), col: 4 (over y, x).
Axes of the slice: x: 2, y: 2, z: 4, core: 2. Of those that a mesh axis runs over, the one named last changes fastest.
Arguments:
- mode_basis: bfloat16 [4096, 4096], P('row'), may hold values from -0.125 to 0.125
- node_coords: float32 [3, 4096], P(None, 'row'), may hold values from -1 to 1
- quad_weights: float32 [4096], P('row'), may hold values from 0.3 to 3
- magnetization: bfloat16 [2, 4096, 32], P(None, 'col', 'row'), may hold values from -6 to 6
- decay_rates: float32 [4096], replicated, may hold values from 0.02 to 1.5
- directions: float32 [6, 3, 32], replicated, may hold values from -3 to 3
Outputs:
- final_magnet: bfloat16 [2, 4096, 32], P(None, 'col', 'row')
All inputs are finite; a program needn't handle non-finite values.
Results may differ from a plain program's by a relative error of at most 0.03.
Values may be sent and summed in bfloat16 or wider, within the bound.
A program may use at most 64 MiB of HBM per device.

v0:
```python
import functools

import jax
import jax.numpy as jnp
from jax import lax
from jax.experimental import pallas as pl
from jax.experimental.pallas import tpu as pltpu
from jax.sharding import PartitionSpec as P

STEPS = 3
MESH = pl.DeviceIdType.MESH
NT = (((1,), (1,)), ((), ()))
NN = (((1,), (0,)), ((), ()))


def kernel(
    R, C, basis_hbm, coords, quad, start, rates, dirs, out,
    basis, landed, joined, modes, parts, sums, weights, scaled, field, lastout, lastin,
    basis_sem, first_send, first_recv, sum_send, sum_recv, mode_send, mode_recv,
    last_send, last_recv,
):
    H = R // C
    r = lax.axis_index("row")
    c = lax.axis_index("col")
    wl = start.shape[1]
    rows = H * 2 * wl
    own = modes.shape[2]
    halves = 2 * STEPS

    basis_copy = pltpu.make_async_copy(basis_hbm, basis, basis_sem)
    basis_copy.start()

    barrier = pltpu.get_barrier_semaphore()
    home = r // H
    for d in range(1, R):
        pl.semaphore_signal(barrier, inc=1, device_id=((r ^ d), c), device_id_type=MESH)
    is_self = home == c

    def greet(row, col):
        @pl.when(jnp.logical_not((row == r) & (col == c)))
        def _():
            pl.semaphore_signal(barrier, inc=1, device_id=(row, col), device_id_type=MESH)

    for t in range(R):
        greet(jnp.int32(t), home)
    for h in range(H):
        for q in range(C):
            greet(H * c + h, jnp.int32(q))
    pl.semaphore_wait(barrier, 3 * R - 1 - 2 * is_self.astype(jnp.int32))

    slot = lax.rem(r, H) * C + c

    def first_copy(t):
        return pltpu.make_async_remote_copy(
            src_ref=start, dst_ref=landed.at[slot], send_sem=first_send.at[t],
            recv_sem=first_recv.at[slot], device_id=(jnp.int32(t), home), device_id_type=MESH,
        )

    def not_self(t):
        return jnp.logical_not((r == t) & is_self)

    for t in range(R):
        @pl.when(not_self(t))
        def _():
            first_copy(t).start()

    @pl.when(is_self)
    def _():
        pltpu.make_async_copy(start, landed.at[slot], first_recv.at[slot]).start()

    row_id = lax.broadcasted_iota(jnp.int32, (rows, dirs.shape[2]), 0)
    wave_id = lax.broadcasted_iota(jnp.int32, (rows, dirs.shape[2]), 1)
    wave = c * (H * wl) + (row_id // (2 * wl)) * wl + row_id % wl
    chosen = wave_id == wave
    for a in range(halves):
        column = [
            jnp.sum(jnp.where(chosen, dirs[a, k : k + 1, :], 0.0), axis=1, keepdims=True)
            for k in range(3)
        ]
        for i in range(quad.shape[0]):
            lanes = pl.ds(i * 128, 128)
            q = quad[i : i + 1, :]
            weights[a, :, lanes] = (
                column[0] * (coords[0:1, lanes] * q)
                + column[1] * (coords[1:2, lanes] * q)
                + column[2] * (coords[2:3, lanes] * q)
            )

    width = start.shape[2]
    for h in range(H):
        for q in range(C):
            pltpu.make_async_copy(start, landed.at[h * C + q], first_recv.at[h * C + q]).wait()
            for x in range(2):
                joined[pl.ds((h * 2 + x) * wl, wl), pl.ds(q * width, width)] = landed[
                    h * C + q, x
                ].astype(jnp.float32)
    basis_copy.wait()

    near = list(range(R))

    def block(t):
        return pl.ds(pl.multiple_of(t * own, own), own)

    part_id = (lax.broadcasted_iota(jnp.int32, (rows, coords.shape[1]), 0) // wl) % 2

    def scale(total, a):
        v = total * weights[a]
        turned = jnp.where(part_id == 0, pltpu.roll(v, rows - wl, 0), -pltpu.roll(v, wl, 0))
        scaled[...] = turned.astype(jnp.bfloat16)

    total = jnp.zeros((rows, coords.shape[1]), jnp.float32)
    for d in near:
        t = (r ^ d)
        piece = joined[:, block(t)]
        if d == 0:
            field[...] = piece
        piece = piece.astype(jnp.bfloat16)
        if d == 0:
            modes[0] = piece
        total = total + lax.dot_general(
            piece, basis[:, block(t)], NT, preferred_element_type=jnp.float32
        )
    scale(total, 0)

    def sum_copy(d):
        return pltpu.make_async_remote_copy(
            src_ref=parts.at[d], dst_ref=sums.at[d], send_sem=sum_send.at[d],
            recv_sem=sum_recv.at[d], device_id=((r ^ d), c), device_id_type=MESH,
        )

    def mode_copy(d):
        return pltpu.make_async_remote_copy(
            src_ref=modes.at[0], dst_ref=modes.at[d], send_sem=mode_send.at[d],
            recv_sem=mode_recv.at[d], device_id=((r ^ d), c), device_id_type=MESH,
        )

    def own_block(factor, keep):
        v = scaled[...]
        for d in reversed(near[1:]):
            t = (r ^ d)
            parts[d] = lax.dot_general(
                v, basis[:, block(t)], NN, preferred_element_type=jnp.float32
            ).astype(jnp.bfloat16)
            sum_copy(d).start()
        acc = lax.dot_general(v, basis[:, block(r)], NN, preferred_element_type=jnp.float32)
        for d in near[1:]:
            sum_copy(d).wait_recv()
            acc = acc + sums[d].astype(jnp.float32)
        lam = jnp.concatenate(
            [rates[pl.ds(r * (own // 128) + i, 1), :] for i in range(own // 128)], axis=1
        )
        return factor * acc + (keep - factor * lam) * modes[0].astype(jnp.float32)

    def half_step(i, carry):
        odd = lax.rem(i, 2) == 1
        factor = jnp.where(odd, 1.0, 0.5).astype(jnp.float32)
        keep = jnp.where(odd, 0.0, 1.0).astype(jnp.float32)
        fresh = own_block(factor, keep)
        fresh = fresh + (1.0 - keep) * field[...]
        rounded = fresh.astype(jnp.bfloat16)
        modes[0] = rounded
        for d in reversed(near[1:]):
            mode_copy(d).start()

        @pl.when(odd)
        def _():
            field[...] = rounded.astype(jnp.float32)

        total = lax.dot_general(
            rounded, basis[:, block(r)], NT, preferred_element_type=jnp.float32
        )
        for d in near[1:]:
            mode_copy(d).wait_recv()
            total = total + lax.dot_general(
                modes[d], basis[:, block((r ^ d))], NT,
                preferred_element_type=jnp.float32,
            )
        scale(total, i + 1)
        for d in near[1:]:
            sum_copy(d).wait_send()
        for d in near[1:]:
            mode_copy(d).wait_send()
        return carry

    lax.fori_loop(0, halves - 1, half_step, 0)

    fresh = own_block(1.0, 0.0) + field[...]
    target_col = r // H
    q = lax.rem(r, H)

    def last_copy(h):
        return pltpu.make_async_remote_copy(
            src_ref=lastout.at[h], dst_ref=lastin.at[q], send_sem=last_send.at[h],
            recv_sem=last_recv.at[q], device_id=(H * c + h, target_col), device_id_type=MESH,
        )

    for h in range(H):
        for x in range(2):
            first = (h * 2 + x) * wl
            lastout[h, x] = fresh[first : first + wl, :].astype(jnp.bfloat16)
        local = (H * c + h == r) & (target_col == c)

        @pl.when(jnp.logical_not(local))
        def _():
            last_copy(h).start()

        @pl.when(local)
        def _():
            pltpu.make_async_copy(lastout.at[h], lastin.at[q], last_recv.at[q]).start()

    for s in range(H):
        pltpu.make_async_copy(lastout.at[0], lastin.at[s], last_recv.at[s]).wait()
        out[:, :, pl.ds(s * own, own)] = lastin[s]
    for d in near[1:]:
        sum_copy(d).wait_send()
    for h in range(H):
        @pl.when(jnp.logical_not((H * c + h == r) & (target_col == c)))
        def _():
            last_copy(h).wait_send()
    for t in range(R):
        @pl.when(not_self(t))
        def _():
            first_copy(t).wait_send()


def on_device(R, C, basis, coords, quad, magnetization, rates, dirs):
    H = R // C
    nodes, mode_count = basis.shape
    start = jnp.transpose(magnetization, (0, 2, 1))
    _, wl, width = start.shape
    rows = H * 2 * wl
    own = mode_count // R
    vmem = pl.BlockSpec(memory_space=pltpu.VMEM)
    dma = pltpu.SemaphoreType.DMA
    bf16, f32 = jnp.bfloat16, jnp.float32
    result = pl.pallas_call(
        functools.partial(kernel, R, C),
        out_shape=jax.ShapeDtypeStruct(start.shape, bf16),
        in_specs=[pl.BlockSpec(memory_space=pl.ANY)] + [vmem] * 5,
        out_specs=vmem,
        scratch_shapes=[
            pltpu.VMEM((nodes, mode_count), bf16),
            pltpu.VMEM((H * C, 2, wl, width), bf16),
            pltpu.VMEM((rows, mode_count), f32),
            pltpu.VMEM((R, rows, own), bf16),
            pltpu.VMEM((R, rows, own), bf16),
            pltpu.VMEM((R, rows, own), bf16),
            pltpu.VMEM((2 * STEPS, rows, nodes), f32),
            pltpu.VMEM((rows, nodes), bf16),
            pltpu.VMEM((rows, own), f32),
            pltpu.VMEM((H, 2, wl, own), bf16),
            pltpu.VMEM((H, 2, wl, own), bf16),
            dma,
            dma((R,)), dma((H * C,)),
            dma((R,)), dma((R,)), dma((R,)), dma((R,)),
            dma((H,)), dma((H,)),
        ],
        compiler_params=pltpu.CompilerParams(collective_id=0, has_side_effects=True),
    )(basis, coords, quad.reshape(-1, 128), start, rates.reshape(-1, 128), dirs)
    return jnp.transpose(result, (0, 2, 1))


def solution(mesh):
    return jax.shard_map(
        functools.partial(on_device, mesh.shape["row"], mesh.shape["col"]),
        mesh=mesh,
        in_specs=(P("row", None), P(None, "row"), P("row"), P(None, "col", "row"), P(), P()),
        out_specs=P(None, "col", "row"),
        check_vma=False,
    )
```

profile of v0, /device:TPU:7, one launch (start us, length us, event | category | flops | bytes accessed | tf_op | source)
XLA Modules:
  0.0 71.8 jit_solution(12201486755956610321)
XLA Ops:
  0.0 70.5 %shard_map.64 = bf16[2,4,1024]{2,1,0:T(4,128)(2,1)} custom-call(bf16[512,4096]{1,0:T(8,128)(2,1)} %basis_hbm.1, f32[3,512]{1,0:T(4,128)} %coords.1, f32[4,128]{1,0:T(4,128)} %bitcast.7, bf16[2,4,1024]{2,1,0:T(4,128)(2,1)} %bitcast.5, f32[32,128]{1,0:T(8,128)} %bitcast.6, f32[6,3,32]{2,1,0:T(4,128)} %dirs.1), custom_call_target="tpu_custom_call" | custom-call | tf_op jit(solution)/shard_map/pallas_call | solution.py:236
  70.5 1.3 %copy.8 = bf16[2,1024,4]{1,2,0:T(4,128)(2,1)} copy(bf16[2,1024,4]{1,2,0:T(4,128)(2,1)} %bitcast.4) | data formatting | bytes 32768
where the time goes:
time: 72.1 us; the launch traced here: 71.8 us
  Pallas kernels  70.5 us (98%)
  local copies, waits for them, and re-layouts  1.33 us (2%)
    pallas_call x1, Pallas kernels, on_device(): pl.pallas_call(functools.partial(kernel, R, C), out_shape=jax.ShapeDtypeS...  70.5 us

commit v1 on v0

v1 whole, which is shorter than its diff:
```python
import functools

import jax
import jax.numpy as jnp
from jax import lax
from jax.experimental import pallas as pl
from jax.experimental.pallas import tpu as pltpu
from jax.sharding import PartitionSpec as P

STEPS = 3
CHUNK = 512
SLAB_PIECES = 4
MESH = pl.DeviceIdType.MESH
NT = (((1,), (1,)), ((), ()))
NN = (((1,), (0,)), ((), ()))


def kernel(
    R, C, basis_hbm, coords, quad, start, rates, dirs, out,
    basis, landed, cur, field, lam, parts, recv, weights, coords_in, quad_in, scaled,
    lastout, lastin,
    basis_sem, slab_send, slab_recv, geo_send, geo_recv, first_send, first_recv,
    part_send, part_recv, last_send, last_recv,
):
    H = R // C
    G = R // H
    r = lax.axis_index("row")
    c = lax.axis_index("col")
    z = r // H
    q = lax.rem(r, H)
    wl, width = start.shape[1], start.shape[2]
    rows = 2 * wl
    local = basis_hbm.shape[0]
    M = basis_hbm.shape[1]
    halves = 2 * STEPS
    chunks = M // CHUNK

    own_copy = pltpu.make_async_copy(basis_hbm, basis.at[pl.ds(0, local), :], basis_sem)
    own_copy.start()

    barrier = pltpu.get_barrier_semaphore()
    is_self = z == c

    def greet(row, col):
        pl.semaphore_signal(barrier, inc=1, device_id=(row, col), device_id_type=MESH)

    def unless(cond, fn):
        pl.when(jnp.logical_not(cond))(fn)

    for d in reversed(range(C)):
        unless(is_self & (d == 0), functools.partial(greet, H * c + q, c ^ d))
    for d in reversed(range(G)):
        unless(is_self & (d == 0), functools.partial(greet, H * (z ^ d) + q, z))
    for d in range(1, G):
        greet(H * (z ^ d) + q, c)
    for d in range(1, H):
        greet(H * z + (q ^ d), c)

    row_id = lax.broadcasted_iota(jnp.int32, (rows, dirs.shape[2]), 0)
    wave_id = lax.broadcasted_iota(jnp.int32, (rows, dirs.shape[2]), 1)
    chosen = wave_id == (H * c + q) * wl + row_id % wl

    def fill_weights(slot, xyz, qw):
        for a in range(halves):
            column = [
                (1.0 if a % 2 else 0.5)
                * jnp.sum(jnp.where(chosen, dirs[a, k : k + 1, :], 0.0), axis=1, keepdims=True)
                for k in range(3)
            ]
            for i in range(local // 128):
                lanes = pl.ds(i * 128, 128)
                w = qw[i : i + 1, :]
                weights[a, :, pl.ds(slot * local + i * 128, 128)] = (
                    column[0] * (xyz[0:1, lanes] * w)
                    + column[1] * (xyz[1:2, lanes] * w)
                    + column[2] * (xyz[2:3, lanes] * w)
                )

    fill_weights(0, coords, quad)
    for i in range(M // 128):
        lam[:, pl.ds(i * 128, 128)] = jnp.broadcast_to(rates[i : i + 1, :], (rows, 128))

    pl.semaphore_wait(barrier, C + 2 * G - 1 + H - 1 - 2 * is_self.astype(jnp.int32))

    def first_copy(d):
        return pltpu.make_async_remote_copy(
            src_ref=start, dst_ref=landed.at[c], send_sem=first_send.at[d],
            recv_sem=first_recv.at[c], device_id=(H * (z ^ d) + q, z), device_id_type=MESH,
        )

    for d in reversed(range(G)):
        unless(is_self & (d == 0), lambda d=d: first_copy(d).start())

    @pl.when(is_self)
    def _():
        pltpu.make_async_copy(start, landed.at[c], first_recv.at[c]).start()

    piece = local // SLAB_PIECES

    def geo_copy(d, which):
        src, dst = ((coords, coords_in), (quad, quad_in))[which]
        return pltpu.make_async_remote_copy(
            src_ref=src, dst_ref=dst.at[d - 1], send_sem=geo_send.at[d - 1, which],
            recv_sem=geo_recv.at[d - 1, which], device_id=(H * z + (q ^ d), c),
            device_id_type=MESH,
        )

    def slab_copy(d, j):
        return pltpu.make_async_remote_copy(
            src_ref=basis_hbm.at[pl.ds(j * piece, piece), :],
            dst_ref=basis.at[pl.ds(d * local + j * piece, piece), :],
            send_sem=slab_send.at[d - 1, j], recv_sem=slab_recv.at[d - 1, j],
            device_id=(H * z + (q ^ d), c), device_id_type=MESH,
        )

    for d in range(1, H):
        for which in range(2):
            geo_copy(d, which).start()
        for j in range(SLAB_PIECES):
            slab_copy(d, j).start()
    for d in range(1, H):
        for which in range(2):
            geo_copy(d, which).wait_recv()
        fill_weights(d, coords_in.at[d - 1], quad_in.at[d - 1])

    for s in range(C):
        pltpu.make_async_copy(start, landed.at[s], first_recv.at[s]).wait()
        for x in range(2):
            field[pl.ds(x * wl, wl), pl.ds(s * width, width)] = landed[s, x].astype(jnp.float32)
    cur[...] = field[...].astype(jnp.bfloat16)
    own_copy.wait()

    part_id = lax.broadcasted_iota(jnp.int32, (rows, local), 0) // wl

    def scale(total, a, slot):
        lanes = pl.ds(slot * local, local)
        v = total * weights[a, :, lanes]
        turned = jnp.where(part_id == 0, pltpu.roll(v, rows - wl, 0), -pltpu.roll(v, wl, 0))
        scaled[:, lanes] = turned.astype(jnp.bfloat16)

    scale(
        lax.dot_general(
            cur[...], basis[pl.ds(0, local), :], NT, preferred_element_type=jnp.float32
        ), 0, 0,
    )
    for d in range(1, H):
        pieces = []
        for j in range(SLAB_PIECES):
            slab_copy(d, j).wait_recv()
            pieces.append(lax.dot_general(
                cur[...], basis[pl.ds(d * local + j * piece, piece), :], NT,
                preferred_element_type=jnp.float32,
            ))
        scale(jnp.concatenate(pieces, axis=1), 0, d)

    def part_copy(p, d, i):
        return pltpu.make_async_remote_copy(
            src_ref=parts.at[p, i], dst_ref=recv.at[p, d - 1, i],
            send_sem=part_send.at[p, d - 1, i], recv_sem=part_recv.at[p, d - 1, i],
            device_id=(H * (z ^ d) + q, c), device_id_type=MESH,
        )

    def half_step(step, carry):
        p = lax.rem(step, 2)
        odd = p == 1
        factor = jnp.where(odd, 1.0, 0.5).astype(jnp.float32)
        v = scaled[...]
        for i in range(chunks):
            parts[p, i] = lax.dot_general(
                v, basis[:, pl.ds(i * CHUNK, CHUNK)], NN, preferred_element_type=jnp.float32
            ).astype(jnp.bfloat16)
            for d in reversed(range(1, G)):
                part_copy(p, d, i).start()
        total = jnp.zeros((rows, H * local), jnp.float32)
        for i in range(chunks):
            lanes = pl.ds(i * CHUNK, CHUNK)
            old = field[:, lanes]
            acc = old - (factor * lam[:, lanes]) * cur[:, lanes].astype(jnp.float32)
            acc = acc + parts[p, i].astype(jnp.float32)
            for d in range(1, G):
                part_copy(p, d, i).wait_recv()
                acc = acc + recv[p, d - 1, i].astype(jnp.float32)
            rounded = acc.astype(jnp.bfloat16)
            cur[:, lanes] = rounded
            field[:, lanes] = jnp.where(odd, rounded.astype(jnp.float32), old)
            total = total + lax.dot_general(
                rounded, basis[:, lanes], NT, preferred_element_type=jnp.float32
            )
        for slot in range(H):
            scale(total[:, slot * local : (slot + 1) * local], step + 1, slot)
        for i in range(chunks):
            for d in range(1, G):
                part_copy(p, d, i).wait_send()
        return carry

    lax.fori_loop(0, halves - 1, half_step, 0)

    def last_copy(d):
        return pltpu.make_async_remote_copy(
            src_ref=lastout.at[d], dst_ref=lastin.at[z], send_sem=last_send.at[d],
            recv_sem=last_recv.at[z], device_id=(H * c + q, c ^ d), device_id_type=MESH,
        )

    v = scaled[...]
    for d in reversed(range(C)):
        lanes = pl.ds(pl.multiple_of((c ^ d) * width, width), width)
        rest = field[:, lanes] - lam[:, lanes] * cur[:, lanes].astype(jnp.float32)
        block = lax.dot_general(v, basis[:, lanes], NN, preferred_element_type=jnp.float32)
        lastout[d] = (block + jnp.where(is_self, rest, 0.0)).astype(jnp.bfloat16)
        if d:
            last_copy(d).start()
    unless(is_self, lambda: last_copy(0).start())

    @pl.when(is_self)
    def _():
        pltpu.make_async_copy(lastout.at[0], lastin.at[z], last_recv.at[z]).start()

    fresh = jnp.zeros((rows, width), jnp.float32)
    for s in range(G):
        pltpu.make_async_copy(lastout.at[0], lastin.at[s], last_recv.at[s]).wait()
        fresh = fresh + lastin[s].astype(jnp.float32)
    for x in range(2):
        out[x] = fresh[x * wl : (x + 1) * wl, :].astype(jnp.bfloat16)

    for d in range(C):
        unless(is_self & (d == 0), lambda d=d: last_copy(d).wait_send())
    for d in range(G):
        unless(is_self & (d == 0), lambda d=d: first_copy(d).wait_send())
    for d in range(1, H):
        for which in range(2):
            geo_copy(d, which).wait_send()
        for j in range(SLAB_PIECES):
            slab_copy(d, j).wait_send()


def on_device(R, C, basis, coords, quad, magnetization, rates, dirs):
    H = R // C
    G = R // H
    local, M = basis.shape
    start = jnp.transpose(magnetization, (0, 2, 1))
    _, wl, width = start.shape
    rows = 2 * wl
    chunks = M // CHUNK
    vmem = pl.BlockSpec(memory_space=pltpu.VMEM)
    dma = pltpu.SemaphoreType.DMA
    bf16, f32 = jnp.bfloat16, jnp.float32
    result = pl.pallas_call(
        functools.partial(kernel, R, C),
        out_shape=jax.ShapeDtypeStruct(start.shape, bf16),
        in_specs=[pl.BlockSpec(memory_space=pl.ANY)] + [vmem] * 5,
        out_specs=vmem,
        scratch_shapes=[
            pltpu.VMEM((H * local, M), bf16),
            pltpu.VMEM((C, 2, wl, width), bf16),
            pltpu.VMEM((rows, M), bf16),
            pltpu.VMEM((rows, M), f32),
            pltpu.VMEM((rows, M), f32),
            pltpu.VMEM((2, chunks, rows, CHUNK), bf16),
            pltpu.VMEM((2, G - 1, chunks, rows, CHUNK), bf16),
            pltpu.VMEM((2 * STEPS, rows, H * local), f32),
            pltpu.VMEM((H - 1, 3, local), f32),
            pltpu.VMEM((H - 1, local // 128, 128), f32),
            pltpu.VMEM((rows, H * local), bf16),
            pltpu.VMEM((C, rows, width), bf16),
            pltpu.VMEM((G, rows, width), bf16),
            dma,
            dma((H - 1, SLAB_PIECES)), dma((H - 1, SLAB_PIECES)),
            dma((H - 1, 2)), dma((H - 1, 2)),
            dma((G,)), dma((C,)),
            dma((2, G - 1, chunks)), dma((2, G - 1, chunks)),
            dma((C,)), dma((G,)),
        ],
        compiler_params=pltpu.CompilerParams(collective_id=0, has_side_effects=True),
    )(basis, coords, quad.reshape(-1, 128), start, rates.reshape(-1, 128), dirs)
    return jnp.transpose(result, (0, 2, 1))


def solution(mesh):
    return jax.shard_map(
        functools.partial(on_device, mesh.shape["row"], mesh.shape["col"]),
        mesh=mesh,
        in_specs=(P("row", None), P(None, "row"), P("row"), P(None, "col", "row"), P(), P()),
        out_specs=P(None, "col", "row"),
        check_vma=False,
    )
```

time: 72.1 us -> 61.5 us (0.85)
  the two profiles are of different devices: /device:TPU:7 before, /device:TPU:0 now
where the time goes in v1:
time: 61.5 us; the launch traced here: 61.2 us
  Pallas kernels  59.8 us (97%)
  local copies, waits for them, and re-layouts  1.33 us (2%)
    pallas_call x1, Pallas kernels, on_device(): pl.pallas_call(functools.partial(kernel, R, C), out_shape=jax.ShapeDtypeS...  59.8 us
    unnamed x1, local copies, waits for them, and re-layouts  1.33 us

profile of v1, /device:TPU:0, one launch (start us, length us, event | category | flops | bytes accessed | tf_op | source)
XLA Modules:
  0.0 61.2 jit_solution(1481636283901140400)
XLA Ops:
  0.0 59.8 %shard_map.64 = bf16[2,4,1024]{2,1,0:T(4,128)(2,1)} custom-call(bf16[512,4096]{1,0:T(8,128)(2,1)} %basis_hbm.1, f32[3,512]{1,0:T(4,128)} %coords.1, f32[4,128]{1,0:T(4,128)} %bitcast.7, bf16[2,4,1024]{2,1,0:T(4,128)(2,1)} %bitcast.5, f32[32,128]{1,0:T(8,128)} %bitcast.6, f32[6,3,32]{2,1,0:T(4,128)} %dirs.1), custom_call_target="tpu_custom_call" | custom-call | tf_op jit(solution)/shard_map/pallas_call | solution.py:247
  59.8 1.3 %copy.8 = bf16[2,1024,4]{1,2,0:T(4,128)(2,1)} copy(bf16[2,1024,4]{1,2,0:T(4,128)(2,1)} %bitcast.4) | data formatting | bytes 32768

commit v2 on v1

v2 whole, which is shorter than its diff:
```python
import functools

import jax
import jax.numpy as jnp
from jax import lax
from jax.experimental import pallas as pl
from jax.experimental.pallas import tpu as pltpu
from jax.sharding import PartitionSpec as P

STEPS = 3
CHUNK = 512
MESH = pl.DeviceIdType.MESH
NT = (((1,), (1,)), ((), ()))
NN = (((1,), (0,)), ((), ()))


def kernel(
    R, C, basis_hbm, coords_hbm, quad_hbm, start, rates_hbm, dirs_hbm, out,
    basis, coords, quad, rates, dirs, landed, cur, field, both, lam, early, parts, recv, weights,
    coords_in, quad_in, nodes_out, nodes_in, scaled, lastout, lastin,
    load_sem, slab_send, slab_recv, geo_send, geo_recv, first_send, first_recv,
    node_send, node_recv, part_send, part_recv, last_send, last_recv,
):
    H = R // C
    G = R // H
    r = lax.axis_index("row")
    c = lax.axis_index("col")
    z = r // H
    q = lax.rem(r, H)
    wl, width = start.shape[1], start.shape[2]
    rows = 2 * wl
    local = basis_hbm.shape[0]
    M = basis_hbm.shape[1]
    halves = 2 * STEPS
    chunks = M // CHUNK

    barrier = pltpu.get_barrier_semaphore()
    is_self = z == c

    def greet(row, col):
        pl.semaphore_signal(barrier, inc=1, device_id=(row, col), device_id_type=MESH)

    def unless(cond, fn):
        pl.when(jnp.logical_not(cond))(fn)

    for d in reversed(range(C)):
        for e in range(H):
            unless(is_self & (d + e == 0), functools.partial(greet, H * c + (q ^ e), c ^ d))
    for d in reversed(range(G)):
        for e in range(H):
            unless(is_self & (d + e == 0), functools.partial(greet, H * (z ^ d) + (q ^ e), z))
    for d in range(1, G):
        greet(H * (z ^ d) + q, c)
    for e in range(1, H):
        greet(H * z + (q ^ e), c)

    loads = [
        pltpu.make_async_copy(src, dst, load_sem.at[k])
        for k, (src, dst) in enumerate((
            (coords_hbm, coords), (quad_hbm, quad), (rates_hbm, rates), (dirs_hbm, dirs),
            (basis_hbm, basis.at[pl.ds(0, local), :]),
        ))
    ]
    for load in loads:
        load.start()
    for load in loads[:-1]:
        load.wait()

    row_id = lax.broadcasted_iota(jnp.int32, (rows, dirs.shape[2]), 0)
    wave_id = lax.broadcasted_iota(jnp.int32, (rows, dirs.shape[2]), 1)
    chosen = wave_id == (H * c + q) * wl + row_id % wl

    def fill_weights(slot, xyz, qw):
        for a in range(halves):
            column = [
                (1.0 if a % 2 else 0.5)
                * jnp.sum(jnp.where(chosen, dirs[a, k : k + 1, :], 0.0), axis=1, keepdims=True)
                for k in range(3)
            ]
            for i in range(local // 128):
                lanes = pl.ds(i * 128, 128)
                w = qw[i : i + 1, :]
                weights[a, :, pl.ds(slot * local + i * 128, 128)] = (
                    column[0] * (xyz[0:1, lanes] * w)
                    + column[1] * (xyz[1:2, lanes] * w)
                    + column[2] * (xyz[2:3, lanes] * w)
                )

    fill_weights(0, coords, quad)
    for i in range(M // 128):
        lam[:, pl.ds(i * 128, 128)] = jnp.broadcast_to(rates[i : i + 1, :], (rows, 128))
    loads[-1].wait()

    pl.semaphore_wait(barrier, H * C + R + G - 1 + H - 1 - 2 * is_self.astype(jnp.int32))

    def first_copy(d, e):
        return pltpu.make_async_remote_copy(
            src_ref=start, dst_ref=landed.at[e, c], send_sem=first_send.at[d, e],
            recv_sem=first_recv.at[e, c], device_id=(H * (z ^ d) + (q ^ e), z),
            device_id_type=MESH,
        )

    for d in reversed(range(G)):
        for e in reversed(range(H)):
            unless(is_self & (d + e == 0), lambda d=d, e=e: first_copy(d, e).start())

    @pl.when(is_self)
    def _():
        pltpu.make_async_copy(start, landed.at[0, c], first_recv.at[0, c]).start()

    def to_core(e, src, dst, send, recv_sem):
        return pltpu.make_async_remote_copy(
            src_ref=src, dst_ref=dst, send_sem=send, recv_sem=recv_sem,
            device_id=(H * z + (q ^ e), c), device_id_type=MESH,
        )

    def geo_copy(e, which):
        src, dst = ((coords, coords_in), (quad, quad_in))[which]
        return to_core(
            e, src, dst.at[e - 1], geo_send.at[e - 1, which], geo_recv.at[e - 1, which]
        )

    def slab_copy(e, i):
        lanes = pl.ds(i * CHUNK, CHUNK)
        return to_core(
            e, basis.at[pl.ds(0, local), lanes], basis.at[pl.ds(e * local, local), lanes],
            slab_send.at[e - 1, i], slab_recv.at[e - 1, i],
        )

    def node_copy(e):
        return to_core(
            e, nodes_out.at[e - 1], nodes_in.at[e - 1], node_send.at[e - 1], node_recv.at[e - 1]
        )

    for e in range(1, H):
        for which in range(2):
            geo_copy(e, which).start()
    for i in range(chunks):
        for e in range(1, H):
            slab_copy(e, i).start()
    for e in range(1, H):
        for which in range(2):
            geo_copy(e, which).wait_recv()
        fill_weights(e, coords_in.at[e - 1], quad_in.at[e - 1])

    for e in reversed(range(H)):
        for s in range(C):
            pltpu.make_async_copy(start, landed.at[e, s], first_recv.at[e, s]).wait()
            for x in range(2):
                field[pl.ds(e * rows + x * wl, wl), pl.ds(s * width, width)] = landed[
                    e, s, x
                ].astype(jnp.float32)
    both[...] = field[...].astype(jnp.bfloat16)
    cur[...] = field[pl.ds(0, rows), :].astype(jnp.bfloat16)

    part_id = lax.broadcasted_iota(jnp.int32, (rows, local), 0) // wl

    def scale(total, a, slot):
        lanes = pl.ds(slot * local, local)
        v = total * weights[a, :, lanes]
        turned = jnp.where(part_id == 0, pltpu.roll(v, rows - wl, 0), -pltpu.roll(v, wl, 0))
        scaled[:, lanes] = turned.astype(jnp.bfloat16)

    total = lax.dot_general(
        both[...], basis[pl.ds(0, local), :], NT, preferred_element_type=jnp.float32
    )
    for e in range(1, H):
        nodes_out[e - 1] = total[e * rows : (e + 1) * rows, :]
        node_copy(e).start()
    scale(total[:rows, :], 0, 0)

    def part_copy(p, d, i):
        return pltpu.make_async_remote_copy(
            src_ref=parts.at[p, i], dst_ref=recv.at[p, d - 1, i],
            send_sem=part_send.at[p, d - 1, i], recv_sem=part_recv.at[p, d - 1, i],
            device_id=(H * (z ^ d) + q, c), device_id_type=MESH,
        )

    def send_part(p, i, block):
        parts[p, i] = block.astype(jnp.bfloat16)
        for d in reversed(range(1, G)):
            part_copy(p, d, i).start()

    def chunk_of(i):
        return pl.ds(i * CHUNK, CHUNK)

    for i in range(chunks):
        early[:, chunk_of(i)] = lax.dot_general(
            scaled[:, pl.ds(0, local)], basis[pl.ds(0, local), chunk_of(i)], NN,
            preferred_element_type=jnp.float32,
        )
    for e in range(1, H):
        node_copy(e).wait_recv()
        scale(nodes_in[e - 1], 0, e)
    for i in range(chunks):
        for e in range(1, H):
            slab_copy(e, i).wait_recv()
        send_part(0, i, early[:, chunk_of(i)] + lax.dot_general(
            scaled[:, pl.ds(local, (H - 1) * local)],
            basis[pl.ds(local, (H - 1) * local), chunk_of(i)], NN,
            preferred_element_type=jnp.float32,
        ))

    def finish(step):
        p = lax.rem(step, 2)
        odd = p == 1
        factor = jnp.where(odd, 1.0, 0.5).astype(jnp.float32)
        total = jnp.zeros((rows, H * local), jnp.float32)
        for i in range(chunks):
            lanes = chunk_of(i)
            old = field[pl.ds(0, rows), lanes]
            acc = old - (factor * lam[:, lanes]) * cur[:, lanes].astype(jnp.float32)
            acc = acc + parts[p, i].astype(jnp.float32)
            for d in range(1, G):
                part_copy(p, d, i).wait_recv()
                acc = acc + recv[p, d - 1, i].astype(jnp.float32)
            rounded = acc.astype(jnp.bfloat16)
            cur[:, lanes] = rounded
            field[pl.ds(0, rows), lanes] = jnp.where(odd, rounded.astype(jnp.float32), old)
            total = total + lax.dot_general(
                rounded, basis[:, lanes], NT, preferred_element_type=jnp.float32
            )
        for slot in range(H):
            scale(total[:, slot * local : (slot + 1) * local], step + 1, slot)

    def sent(p):
        for i in range(chunks):
            for d in range(1, G):
                part_copy(p, d, i).wait_send()

    def half_step(step, carry):
        finish(step)
        p = lax.rem(step, 2)
        v = scaled[...]
        for i in range(chunks):
            send_part(1 - p, i, lax.dot_general(
                v, basis[:, chunk_of(i)], NN, preferred_element_type=jnp.float32
            ))
        sent(p)
        return carry

    lax.fori_loop(0, halves - 2, half_step, 0)
    finish(halves - 2)

    def last_copy(d):
        return pltpu.make_async_remote_copy(
            src_ref=lastout.at[d], dst_ref=lastin.at[z], send_sem=last_send.at[d],
            recv_sem=last_recv.at[z], device_id=(H * c + q, c ^ d), device_id_type=MESH,
        )

    v = scaled[...]
    for d in reversed(range(C)):
        lanes = pl.ds(pl.multiple_of((c ^ d) * width, width), width)
        rest = field[pl.ds(0, rows), lanes] - lam[:, lanes] * cur[:, lanes].astype(jnp.float32)
        block = lax.dot_general(v, basis[:, lanes], NN, preferred_element_type=jnp.float32)
        lastout[d] = (block + jnp.where(is_self, rest, 0.0)).astype(jnp.bfloat16)
        if d:
            last_copy(d).start()
    unless(is_self, lambda: last_copy(0).start())

    @pl.when(is_self)
    def _():
        pltpu.make_async_copy(lastout.at[0], lastin.at[z], last_recv.at[z]).start()

    fresh = jnp.zeros((rows, width), jnp.float32)
    for s in range(G):
        pltpu.make_async_copy(lastout.at[0], lastin.at[s], last_recv.at[s]).wait()
        fresh = fresh + lastin[s].astype(jnp.float32)
    for x in range(2):
        out[x] = fresh[x * wl : (x + 1) * wl, :].astype(jnp.bfloat16)

    sent((halves - 2) % 2)
    for d in range(C):
        unless(is_self & (d == 0), lambda d=d: last_copy(d).wait_send())
    for d in range(G):
        for e in range(H):
            unless(is_self & (d + e == 0), lambda d=d, e=e: first_copy(d, e).wait_send())
    for e in range(1, H):
        node_copy(e).wait_send()
        for which in range(2):
            geo_copy(e, which).wait_send()
        for i in range(chunks):
            slab_copy(e, i).wait_send()


def on_device(R, C, basis, coords, quad, magnetization, rates, dirs):
    H = R // C
    G = R // H
    local, M = basis.shape
    start = jnp.transpose(magnetization, (0, 2, 1))
    quad = quad.reshape(-1, 128)
    rates = rates.reshape(-1, 128)
    _, wl, width = start.shape
    rows = 2 * wl
    chunks = M // CHUNK
    dma = pltpu.SemaphoreType.DMA
    bf16, f32 = jnp.bfloat16, jnp.float32
    result = pl.pallas_call(
        functools.partial(kernel, R, C),
        out_shape=jax.ShapeDtypeStruct(start.shape, bf16),
        in_specs=[pl.BlockSpec(memory_space=pl.ANY)] * 6,
        out_specs=pl.BlockSpec(memory_space=pltpu.VMEM),
        scratch_shapes=[
            pltpu.VMEM((H * local, M), bf16),
            pltpu.VMEM(coords.shape, f32),
            pltpu.VMEM(quad.shape, f32),
            pltpu.VMEM(rates.shape, f32),
            pltpu.VMEM(dirs.shape, f32),
            pltpu.VMEM((H, C, 2, wl, width), bf16),
            pltpu.VMEM((rows, M), bf16),
            pltpu.VMEM((H * rows, M), f32),
            pltpu.VMEM((H * rows, M), bf16),
            pltpu.VMEM((rows, M), f32),
            pltpu.VMEM((rows, M), f32),
            pltpu.VMEM((2, chunks, rows, CHUNK), bf16),
            pltpu.VMEM((2, G - 1, chunks, rows, CHUNK), bf16),
            pltpu.VMEM((2 * STEPS, rows, H * local), f32),
            pltpu.VMEM((H - 1,) + coords.shape, f32),
            pltpu.VMEM((H - 1,) + quad.shape, f32),
            pltpu.VMEM((H - 1, rows, local), f32),
            pltpu.VMEM((H - 1, rows, local), f32),
            pltpu.VMEM((rows, H * local), bf16),
            pltpu.VMEM((C, rows, width), bf16),
            pltpu.VMEM((G, rows, width), bf16),
            dma((5,)),
            dma((H - 1, chunks)), dma((H - 1, chunks)),
            dma((H - 1, 2)), dma((H - 1, 2)),
            dma((G, H)), dma((H, C)),
            dma((H - 1,)), dma((H - 1,)),
            dma((2, G - 1, chunks)), dma((2, G - 1, chunks)),
            dma((C,)), dma((G,)),
        ],
        compiler_params=pltpu.CompilerParams(collective_id=0, has_side_effects=True),
    )(basis, coords, quad, start, rates, dirs)
    return jnp.transpose(result, (0, 2, 1))


def solution(mesh):
    return jax.shard_map(
        functools.partial(on_device, mesh.shape["row"], mesh.shape["col"]),
        mesh=mesh,
        in_specs=(P("row", None), P(None, "row"), P("row"), P(None, "col", "row"), P(), P()),
        out_specs=P(None, "col", "row"),
        check_vma=False,
    )
```

time: 61.5 us -> 59.8 us (0.972)
  Pallas kernels: 59.8 us -> 58.2 us
    pallas_call x1, Pallas kernels: 59.8 us -> 58.2 us  [on_device(): pl.pallas_call(functools.partial(kernel, R, C), out_shape=jax.ShapeDtypeS...]
where the time goes in v2:
time: 59.8 us; the launch traced here: 59.5 us
  Pallas kernels  58.2 us (97%)
  local copies, waits for them, and re-layouts  1.33 us (2%)
    pallas_call x1, Pallas kernels, on_device(): pl.pallas_call(functools.partial(kernel, R, C), out_shape=jax.ShapeDtypeS...  58.2 us
    unnamed x1, local copies, waits for them, and re-layouts  1.33 us

profile of v2, /device:TPU:0, one launch (start us, length us, event | category | flops | bytes accessed | tf_op | source)
XLA Modules:
  0.0 59.5 jit_solution(7335468522830309158)
XLA Ops:
  0.0 58.2 %shard_map.64 = bf16[2,4,1024]{2,1,0:T(4,128)(2,1)} custom-call(bf16[512,4096]{1,0:T(8,128)(2,1)} %basis_hbm.1, f32[3,512]{1,0:T(4,128)} %coords_hbm.1, f32[4,128]{1,0:T(4,128)} %bitcast.7, bf16[2,4,1024]{2,1,0:T(4,128)(2,1)} %bitcast.5, f32[32,128]{1,0:T(8,128)} %bitcast.6, f32[6,3,32]{2,1,0:T(4,128)} %dirs_hbm.1), custom_call_target="tpu_custom_call" | custom-call | tf_op jit(solution)/shard_map/pallas_call | solution.py:298
  58.2 1.3 %copy.8 = bf16[2,1024,4]{1,2,0:T(4,128)(2,1)} copy(bf16[2,1024,4]{1,2,0:T(4,128)(2,1)} %bitcast.4) | data formatting | bytes 32768

commit v3 on v2

--- a/solution.py
+++ b/solution.py
@@ -8,15 +8,20 @@
 from jax.sharding import PartitionSpec as P
 
 STEPS = 3
-CHUNK = 512
+CHUNKS = (512,) * 8
 MESH = pl.DeviceIdType.MESH
 NT = (((1,), (1,)), ((), ()))
 NN = (((1,), (0,)), ((), ()))
 
 
+def cuts_of(M):
+    starts = [sum(CHUNKS[:i]) for i in range(len(CHUNKS))]
+    return list(zip(starts, CHUNKS))
+
+
 def kernel(
     R, C, basis_hbm, coords_hbm, quad_hbm, start, rates_hbm, dirs_hbm, out,
-    basis, coords, quad, rates, dirs, landed, cur, field, both, lam, early, parts, recv, weights,
+    basis, coords, quad, rates, dirs, landed, cur, field, ready, lam, early, parts, recv, weights,
     coords_in, quad_in, nodes_out, nodes_in, scaled, lastout, lastin,
     load_sem, slab_send, slab_recv, geo_send, geo_recv, first_send, first_recv,
     node_send, node_recv, part_send, part_recv, last_send, last_recv,
@@ -32,7 +37,8 @@
     local = basis_hbm.shape[0]
     M = basis_hbm.shape[1]
     halves = 2 * STEPS
-    chunks = M // CHUNK
+    cuts = cuts_of(M)
+    chunks = len(cuts)
 
     barrier = pltpu.get_barrier_semaphore()
     is_self = z == c
@@ -120,8 +126,11 @@
             e, src, dst.at[e - 1], geo_send.at[e - 1, which], geo_recv.at[e - 1, which]
         )
 
+    def chunk_of(i):
+        return pl.ds(*cuts[i])
+
     def slab_copy(e, i):
-        lanes = pl.ds(i * CHUNK, CHUNK)
+        lanes = chunk_of(i)
         return to_core(
             e, basis.at[pl.ds(0, local), lanes], basis.at[pl.ds(e * local, local), lanes],
             slab_send.at[e - 1, i], slab_recv.at[e - 1, i],
@@ -143,16 +152,6 @@
             geo_copy(e, which).wait_recv()
         fill_weights(e, coords_in.at[e - 1], quad_in.at[e - 1])
 
-    for e in reversed(range(H)):
-        for s in range(C):
-            pltpu.make_async_copy(start, landed.at[e, s], first_recv.at[e, s]).wait()
-            for x in range(2):
-                field[pl.ds(e * rows + x * wl, wl), pl.ds(s * width, width)] = landed[
-                    e, s, x
-                ].astype(jnp.float32)
-    both[...] = field[...].astype(jnp.bfloat16)
-    cur[...] = field[pl.ds(0, rows), :].astype(jnp.bfloat16)
-
     part_id = lax.broadcasted_iota(jnp.int32, (rows, local), 0) // wl
 
     def scale(total, a, slot):
@@ -161,9 +160,19 @@
         turned = jnp.where(part_id == 0, pltpu.roll(v, rows - wl, 0), -pltpu.roll(v, wl, 0))
         scaled[:, lanes] = turned.astype(jnp.bfloat16)
 
-    total = lax.dot_general(
-        both[...], basis[pl.ds(0, local), :], NT, preferred_element_type=jnp.float32
-    )
+    total = jnp.zeros((H * rows, local), jnp.float32)
+    for d in range(C):
+        s = c ^ d
+        lanes = pl.ds(pl.multiple_of(s * width, width), width)
+        for e in range(H):
+            pltpu.make_async_copy(start, landed.at[e, s], first_recv.at[e, s]).wait()
+            for x in range(2):
+                field[pl.ds(e * rows + x * wl, wl), lanes] = landed[e, s, x].astype(jnp.float32)
+        block = field[:, lanes].astype(jnp.bfloat16)
+        cur[:, lanes] = block[:rows, :]
+        total = total + lax.dot_general(
+            block, basis[pl.ds(0, local), lanes], NT, preferred_element_type=jnp.float32
+        )
     for e in range(1, H):
         nodes_out[e - 1] = total[e * rows : (e + 1) * rows, :]
         node_copy(e).start()
@@ -171,18 +180,15 @@
 
     def part_copy(p, d, i):
         return pltpu.make_async_remote_copy(
-            src_ref=parts.at[p, i], dst_ref=recv.at[p, d - 1, i],
+            src_ref=parts.at[p, :, chunk_of(i)], dst_ref=recv.at[p, d - 1, :, chunk_of(i)],
             send_sem=part_send.at[p, d - 1, i], recv_sem=part_recv.at[p, d - 1, i],
             device_id=(H * (z ^ d) + q, c), device_id_type=MESH,
         )
 
     def send_part(p, i, block):
-        parts[p, i] = block.astype(jnp.bfloat16)
+        parts[p, :, chunk_of(i)] = block.astype(jnp.bfloat16)
         for d in reversed(range(1, G)):
             part_copy(p, d, i).start()
-
-    def chunk_of(i):
-        return pl.ds(i * CHUNK, CHUNK)
 
     for i in range(chunks):
         early[:, chunk_of(i)] = lax.dot_general(
@@ -205,18 +211,25 @@
         p = lax.rem(step, 2)
         odd = p == 1
         factor = jnp.where(odd, 1.0, 0.5).astype(jnp.float32)
+        for i in range(chunks):
+            lanes = chunk_of(i)
+            ready[:, lanes] = (
+                field[pl.ds(0, rows), lanes]
+                - (factor * lam[:, lanes]) * cur[:, lanes].astype(jnp.float32)
+                + parts[p, :, lanes].astype(jnp.float32)
+            )
         total = jnp.zeros((rows, H * local), jnp.float32)
         for i in range(chunks):
             lanes = chunk_of(i)
-            old = field[pl.ds(0, rows), lanes]
-            acc = old - (factor * lam[:, lanes]) * cur[:, lanes].astype(jnp.float32)
-            acc = acc + parts[p, i].astype(jnp.float32)
+            acc = ready[:, lanes]
             for d in range(1, G):
                 part_copy(p, d, i).wait_recv()
-                acc = acc + recv[p, d - 1, i].astype(jnp.float32)
+                acc = acc + recv[p, d - 1, :, lanes].astype(jnp.float32)
             rounded = acc.astype(jnp.bfloat16)
             cur[:, lanes] = rounded
-            field[pl.ds(0, rows), lanes] = jnp.where(odd, rounded.astype(jnp.float32), old)
+            field[pl.ds(0, rows), lanes] = jnp.where(
+                odd, rounded.astype(jnp.float32), field[pl.ds(0, rows), lanes]
+            )
             total = total + lax.dot_general(
                 rounded, basis[:, lanes], NT, preferred_element_type=jnp.float32
             )
@@ -292,12 +305,13 @@
     rates = rates.reshape(-1, 128)
     _, wl, width = start.shape
     rows = 2 * wl
-    chunks = M // CHUNK
+    cuts = cuts_of(M)
+    chunks = len(cuts)
     dma = pltpu.SemaphoreType.DMA
     bf16, f32 = jnp.bfloat16, jnp.float32
     result = pl.pallas_call(
         functools.partial(kernel, R, C),
-        out_shape=jax.ShapeDtypeStruct(start.shape, bf16),
+        out_shape=pltpu.VMEM(start.shape, bf16),
         in_specs=[pl.BlockSpec(memory_space=pl.ANY)] * 6,
         out_specs=pl.BlockSpec(memory_space=pltpu.VMEM),
         scratch_shapes=[
@@ -309,11 +323,11 @@
             pltpu.VMEM((H, C, 2, wl, width), bf16),
             pltpu.VMEM((rows, M), bf16),
             pltpu.VMEM((H * rows, M), f32),
-            pltpu.VMEM((H * rows, M), bf16),
             pltpu.VMEM((rows, M), f32),
             pltpu.VMEM((rows, M), f32),
-            pltpu.VMEM((2, chunks, rows, CHUNK), bf16),
-            pltpu.VMEM((2, G - 1, chunks, rows, CHUNK), bf16),
+            pltpu.VMEM((rows, M), f32),
+            pltpu.VMEM((2, rows, M), bf16),
+            pltpu.VMEM((2, G - 1, rows, M), bf16),
             pltpu.VMEM((2 * STEPS, rows, H * local), f32),
             pltpu.VMEM((H - 1,) + coords.shape, f32),
             pltpu.VMEM((H - 1,) + quad.shape, f32),

time: 59.8 us -> 58.3 us (0.975)
  Pallas kernels: 58.2 us -> 57.4 us
  local copies, waits for them, and re-layouts: 1.33 us -> 0.61 us
    pallas_call x1, Pallas kernels: 58.2 us -> 57.4 us  [on_device(): pl.pallas_call(functools.partial(kernel, R, C), out_shape=pltpu.VMEM(star...]
    unnamed x1, local copies, waits for them, and re-layouts: 1.33 us -> 0.61 us
where the time goes in v3:
time: 58.3 us; the launch traced here: 58.1 us
  Pallas kernels  57.4 us (98%)
  local copies, waits for them, and re-layouts  0.61 us (1%)
    pallas_call x1, Pallas kernels, on_device(): pl.pallas_call(functools.partial(kernel, R, C), out_shape=pltpu.VMEM(star...  57.4 us

profile of v3, /device:TPU:0, one launch (start us, length us, event | category | flops | bytes accessed | tf_op | source)
XLA Modules:
  0.0 58.1 jit_solution(3808531065756919482)
XLA Ops:
  0.0 57.4 %shard_map.64 = bf16[2,4,1024]{2,1,0:T(4,128)(2,1)S(1)} custom-call(bf16[512,4096]{1,0:T(8,128)(2,1)} %basis_hbm.1, f32[3,512]{1,0:T(4,128)} %coords_hbm.1, f32[4,128]{1,0:T(4,128)} %bitcast.7, bf16[2,4,1024]{2,1,0:T(4,128)(2,1)} %bitcast.5, f32[32,128]{1,0:T(8,128)} %bitcast.6, f32[6,3,32]{2,1,0:T(4,128)} %dirs_hbm.1), custom_call_target="tpu_custom_call" | custom-call | tf_op jit(solution)/shard_map/pallas_call | solution.py:312
  57.5 0.6 %copy.8 = bf16[2,1024,4]{1,2,0:T(4,128)(2,1)} copy(bf16[2,1024,4]{1,2,0:T(4,128)(2,1)S(1)} %bitcast.4) | data formatting | bytes 32768

commit v4 on v3

--- a/solution.py
+++ b/solution.py
@@ -187,7 +187,7 @@
 
     def send_part(p, i, block):
         parts[p, :, chunk_of(i)] = block.astype(jnp.bfloat16)
-        for d in reversed(range(1, G)):
+        for d in [d for d in reversed(range(1, G)) if d != 2] + [2]:
             part_copy(p, d, i).start()
 
     for i in range(chunks):

time: 58.3 us -> 57.2 us (0.981)
  Pallas kernels: 57.4 us -> 56.4 us
    pallas_call x1, Pallas kernels: 57.4 us -> 56.4 us  [on_device(): pl.pallas_call(functools.partial(kernel, R, C), out_shape=pltpu.VMEM(star...]
where the time goes in v4:
time: 57.2 us; the launch traced here: 57 us
  Pallas kernels  56.4 us (99%)
  local copies, waits for them, and re-layouts  0.61 us (1%)
    pallas_call x1, Pallas kernels, on_device(): pl.pallas_call(functools.partial(kernel, R, C), out_shape=pltpu.VMEM(star...  56.4 us

profile of v4, /device:TPU:0, one launch (start us, length us, event | category | flops | bytes accessed | tf_op | source)
XLA Modules:
  0.0 57.0 jit_solution(2518525713022801343)
XLA Ops:
  0.0 56.4 %shard_map.64 = bf16[2,4,1024]{2,1,0:T(4,128)(2,1)S(1)} custom-call(bf16[512,4096]{1,0:T(8,128)(2,1)} %basis_hbm.1, f32[3,512]{1,0:T(4,128)} %coords_hbm.1, f32[4,128]{1,0:T(4,128)} %bitcast.7, bf16[2,4,1024]{2,1,0:T(4,128)(2,1)} %bitcast.5, f32[32,128]{1,0:T(8,128)} %bitcast.6, f32[6,3,32]{2,1,0:T(4,128)} %dirs_hbm.1), custom_call_target="tpu_custom_call" | custom-call | tf_op jit(solution)/shard_map/pallas_call | solution.py:312
  56.4 0.6 %copy.8 = bf16[2,1024,4]{1,2,0:T(4,128)(2,1)} copy(bf16[2,1024,4]{1,2,0:T(4,128)(2,1)S(1)} %bitcast.4) | data formatting | bytes 32768

commit v5 on v4

--- a/solution.py
+++ b/solution.py
@@ -24,7 +24,7 @@
     basis, coords, quad, rates, dirs, landed, cur, field, ready, lam, early, parts, recv, weights,
     coords_in, quad_in, nodes_out, nodes_in, scaled, lastout, lastin,
     load_sem, slab_send, slab_recv, geo_send, geo_recv, first_send, first_recv,
-    node_send, node_recv, part_send, part_recv, last_send, last_recv,
+    node_send, node_recv, turn, part_send, part_recv, last_send, last_recv,
 ):
     H = R // C
     G = R // H
@@ -187,7 +187,7 @@
 
     def send_part(p, i, block):
         parts[p, :, chunk_of(i)] = block.astype(jnp.bfloat16)
-        for d in [d for d in reversed(range(1, G)) if d != 2] + [2]:
+        for d in [1] + list(reversed(range(2, G))):
             part_copy(p, d, i).start()
 
     for i in range(chunks):
@@ -198,6 +198,10 @@
     for e in range(1, H):
         node_copy(e).wait_recv()
         scale(nodes_in[e - 1], 0, e)
+    @pl.when(q != 0)
+    def _():
+        pl.semaphore_wait(turn, 1)
+
     for i in range(chunks):
         for e in range(1, H):
             slab_copy(e, i).wait_recv()
@@ -206,6 +210,14 @@
             basis[pl.ds(local, (H - 1) * local), chunk_of(i)], NN,
             preferred_element_type=jnp.float32,
         ))
+    for d in range(1, G):
+        part_copy(0, d, chunks - 1).wait_send()
+
+    @pl.when(q != H - 1)
+    def _():
+        pl.semaphore_signal(
+            turn, inc=1, device_id=(H * z + lax.rem(q + 1, H), c), device_id_type=MESH
+        )
 
     def finish(step):
         p = lax.rem(step, 2)
@@ -236,8 +248,8 @@
         for slot in range(H):
             scale(total[:, slot * local : (slot + 1) * local], step + 1, slot)
 
-    def sent(p):
-        for i in range(chunks):
+    def sent(p, count):
+        for i in range(count):
             for d in range(1, G):
                 part_copy(p, d, i).wait_send()
 
@@ -249,7 +261,13 @@
             send_part(1 - p, i, lax.dot_general(
                 v, basis[:, chunk_of(i)], NN, preferred_element_type=jnp.float32
             ))
-        sent(p)
+        sent(p, chunks - 1)
+
+        @pl.when(step > 0)
+        def _():
+            for d in range(1, G):
+                part_copy(p, d, chunks - 1).wait_send()
+
         return carry
 
     lax.fori_loop(0, halves - 2, half_step, 0)
@@ -282,7 +300,7 @@
     for x in range(2):
         out[x] = fresh[x * wl : (x + 1) * wl, :].astype(jnp.bfloat16)
 
-    sent((halves - 2) % 2)
+    sent((halves - 2) % 2, chunks)
     for d in range(C):
         unless(is_self & (d == 0), lambda d=d: last_copy(d).wait_send())
     for d in range(G):
@@ -341,6 +359,7 @@
             dma((H - 1, 2)), dma((H - 1, 2)),
             dma((G, H)), dma((H, C)),
             dma((H - 1,)), dma((H - 1,)),
+            pltpu.SemaphoreType.REGULAR,
             dma((2, G - 1, chunks)), dma((2, G - 1, chunks)),
             dma((C,)), dma((G,)),
         ],

time: 57.2 us -> 56.1 us (0.981)
  Pallas kernels: 56.4 us -> 55.3 us
    pallas_call x1, Pallas kernels: 56.4 us -> 55.3 us  [on_device(): pl.pallas_call(functools.partial(kernel, R, C), out_shape=pltpu.VMEM(star...]
where the time goes in v5:
time: 56.1 us; the launch traced here: 55.9 us
  Pallas kernels  55.3 us (99%)
  local copies, waits for them, and re-layouts  0.61 us (1%)
    pallas_call x1, Pallas kernels, on_device(): pl.pallas_call(functools.partial(kernel, R, C), out_shape=pltpu.VMEM(star...  55.3 us

profile of v5, /device:TPU:0, one launch (start us, length us, event | category | flops | bytes accessed | tf_op | source)
XLA Modules:
  0.0 55.9 jit_solution(14351664646715286457)
XLA Ops:
  0.0 55.3 %shard_map.64 = bf16[2,4,1024]{2,1,0:T(4,128)(2,1)S(1)} custom-call(bf16[512,4096]{1,0:T(8,128)(2,1)} %basis_hbm.1, f32[3,512]{1,0:T(4,128)} %coords_hbm.1, f32[4,128]{1,0:T(4,128)} %bitcast.7, bf16[2,4,1024]{2,1,0:T(4,128)(2,1)} %bitcast.5, f32[32,128]{1,0:T(8,128)} %bitcast.6, f32[6,3,32]{2,1,0:T(4,128)} %dirs_hbm.1), custom_call_target="tpu_custom_call" | custom-call | tf_op jit(solution)/shard_map/pallas_call | solution.py:330
  55.3 0.6 %copy.8 = bf16[2,1024,4]{1,2,0:T(4,128)(2,1)} copy(bf16[2,1024,4]{1,2,0:T(4,128)(2,1)S(1)} %bitcast.4) | data formatting | bytes 32768

commit v6 on v5

--- a/solution.py
+++ b/solution.py
@@ -210,11 +210,10 @@
             basis[pl.ds(local, (H - 1) * local), chunk_of(i)], NN,
             preferred_element_type=jnp.float32,
         ))
-    for d in range(1, G):
-        part_copy(0, d, chunks - 1).wait_send()
-
     @pl.when(q != H - 1)
     def _():
+        for d in range(1, G):
+            part_copy(0, d, chunks - 1).wait_send()
         pl.semaphore_signal(
             turn, inc=1, device_id=(H * z + lax.rem(q + 1, H), c), device_id_type=MESH
         )
@@ -263,7 +262,7 @@
             ))
         sent(p, chunks - 1)
 
-        @pl.when(step > 0)
+        @pl.when((step > 0) | (q == H - 1))
         def _():
             for d in range(1, G):
                 part_copy(p, d, chunks - 1).wait_send()

time: 56.1 us -> 55.6 us (level)
  no operation moved by 1% of the time
where the time goes in v6:
time: 55.6 us; the launch traced here: 55.4 us
  Pallas kernels  54.8 us (99%)
  local copies, waits for them, and re-layouts  0.61 us (1%)
    pallas_call x1, Pallas kernels, on_device(): pl.pallas_call(functools.partial(kernel, R, C), out_shape=pltpu.VMEM(star...  54.8 us

profile of v6, /device:TPU:0, one launch (start us, length us, event | category | flops | bytes accessed | tf_op | source)
XLA Modules:
  0.0 55.4 jit_solution(18104675685689304752)
XLA Ops:
  0.0 54.8 %shard_map.64 = bf16[2,4,1024]{2,1,0:T(4,128)(2,1)S(1)} custom-call(bf16[512,4096]{1,0:T(8,128)(2,1)} %basis_hbm.1, f32[3,512]{1,0:T(4,128)} %coords_hbm.1, f32[4,128]{1,0:T(4,128)} %bitcast.7, bf16[2,4,1024]{2,1,0:T(4,128)(2,1)} %bitcast.5, f32[32,128]{1,0:T(8,128)} %bitcast.6, f32[6,3,32]{2,1,0:T(4,128)} %dirs_hbm.1), custom_call_target="tpu_custom_call" | custom-call | tf_op jit(solution)/shard_map/pallas_call | solution.py:329
  54.8 0.6 %copy.8 = bf16[2,1024,4]{1,2,0:T(4,128)(2,1)} copy(bf16[2,1024,4]{1,2,0:T(4,128)(2,1)S(1)} %bitcast.4) | data formatting | bytes 32768

commit v7 on v6

--- a/solution.py
+++ b/solution.py
@@ -8,15 +8,14 @@
 from jax.sharding import PartitionSpec as P
 
 STEPS = 3
-CHUNKS = (512,) * 8
+CHUNK = 512
 MESH = pl.DeviceIdType.MESH
 NT = (((1,), (1,)), ((), ()))
 NN = (((1,), (0,)), ((), ()))
 
 
 def cuts_of(M):
-    starts = [sum(CHUNKS[:i]) for i in range(len(CHUNKS))]
-    return list(zip(starts, CHUNKS))
+    return [(i * CHUNK, CHUNK) for i in range(M // CHUNK)]
 
 
 def kernel(

time: 55.6 us -> 55.6 us (level)
  no operation moved by 1% of the time
where the time goes in v7:
time: 55.6 us; the launch traced here: 55.4 us
  Pallas kernels  54.8 us (99%)
  local copies, waits for them, and re-layouts  0.61 us (1%)
    pallas_call x1, Pallas kernels, on_device(): pl.pallas_call(functools.partial(kernel, R, C), out_shape=pltpu.VMEM(star...  54.8 us

profile of v7, /device:TPU:0, one launch (start us, length us, event | category | flops | bytes accessed | tf_op | source)
XLA Modules:
  0.0 55.4 jit_solution(18104675685689304752)
XLA Ops:
  0.0 54.8 %shard_map.64 = bf16[2,4,1024]{2,1,0:T(4,128)(2,1)S(1)} custom-call(bf16[512,4096]{1,0:T(8,128)(2,1)} %basis_hbm.1, f32[3,512]{1,0:T(4,128)} %coords_hbm.1, f32[4,128]{1,0:T(4,128)} %bitcast.7, bf16[2,4,1024]{2,1,0:T(4,128)(2,1)} %bitcast.5, f32[32,128]{1,0:T(8,128)} %bitcast.6, f32[6,3,32]{2,1,0:T(4,128)} %dirs_hbm.1), custom_call_target="tpu_custom_call" | custom-call | tf_op jit(solution)/shard_map/pallas_call | solution.py:328
  54.8 0.6 %copy.8 = bf16[2,1024,4]{1,2,0:T(4,128)(2,1)} copy(bf16[2,1024,4]{1,2,0:T(4,128)(2,1)S(1)} %bitcast.4) | data formatting | bytes 32768

commit v8 on v7

--- a/solution.py
+++ b/solution.py
@@ -143,7 +143,8 @@
     for e in range(1, H):
         for which in range(2):
             geo_copy(e, which).start()
-    for i in range(chunks):
+    ahead = chunks // 2
+    for i in range(ahead):
         for e in range(1, H):
             slab_copy(e, i).start()
     for e in range(1, H):
@@ -175,6 +176,9 @@
     for e in range(1, H):
         nodes_out[e - 1] = total[e * rows : (e + 1) * rows, :]
         node_copy(e).start()
+    for i in range(ahead, chunks):
+        for e in range(1, H):
+            slab_copy(e, i).start()
     scale(total[:rows, :], 0, 0)
 
     def part_copy(p, d, i):

time: 55.6 us -> 58.9 us (1.059)
  Pallas kernels: 54.8 us -> 58 us
    pallas_call x1, Pallas kernels: 54.8 us -> 58 us  [on_device(): pl.pallas_call(functools.partial(kernel, R, C), out_shape=pltpu.VMEM(star...]
where the time goes in v8:
time: 58.9 us; the launch traced here: 58.7 us
  Pallas kernels  58 us (98%)
  local copies, waits for them, and re-layouts  0.61 us (1%)
    pallas_call x1, Pallas kernels, on_device(): pl.pallas_call(functools.partial(kernel, R, C), out_shape=pltpu.VMEM(star...  58 us

profile of v8, /device:TPU:0, one launch (start us, length us, event | category | flops | bytes accessed | tf_op | source)
XLA Modules:
  0.0 58.7 jit_solution(347614381927051749)
XLA Ops:
  0.0 58.0 %shard_map.64 = bf16[2,4,1024]{2,1,0:T(4,128)(2,1)S(1)} custom-call(bf16[512,4096]{1,0:T(8,128)(2,1)} %basis_hbm.1, f32[3,512]{1,0:T(4,128)} %coords_hbm.1, f32[4,128]{1,0:T(4,128)} %bitcast.7, bf16[2,4,1024]{2,1,0:T(4,128)(2,1)} %bitcast.5, f32[32,128]{1,0:T(8,128)} %bitcast.6, f32[6,3,32]{2,1,0:T(4,128)} %dirs_hbm.1), custom_call_target="tpu_custom_call" | custom-call | tf_op jit(solution)/shard_map/pallas_call | solution.py:332
  58.1 0.6 %copy.8 = bf16[2,1024,4]{1,2,0:T(4,128)(2,1)} copy(bf16[2,1024,4]{1,2,0:T(4,128)(2,1)S(1)} %bitcast.4) | data formatting | bytes 32768
